TPU v7x, 32 devices: a whole 2x2x4 slice. The times are simulated.
32 devices in a mesh: row: 8 (over y, x, core), col: 4 (over z).
Axes of the slice: x: 2, y: 2, z: 4, core: 2. Of those that a mesh axis runs over, the one named last changes fastest.
Arguments:
- a_blocks: bfloat16 [3328, 128, 128], P(('row', 'col')), may hold values from -6 to 6
- a_coord: int32 [3328, 2], P(('row', 'col')), may hold values from 0 to 111, as said below
- b_blocks: bfloat16 [1664, 128, 128], P(('row', 'col')), may hold values from -0.099609375 to 0.099609375
- b_coord: int32 [1664, 2], P(('row', 'col')), may hold values from 0 to 55, as said below
- c_keep: int32 [112, 56], P('row', 'col'), may hold values 0 or 1
Outputs:
- c_window: bfloat16 [14336, 7168], P('row', 'col')
Inputs may be any that keep to these rules, and one draw needn't show every extreme that they name: `a_coord`: every row names a distinct block of dense_a. A block (I, K) belongs to the device of grid row I // 14 and grid column (K // 8 - I // 14) mod 4; among the 104 rows of one device, at most 4 name blocks of the same device, and every device that is named at all is named exactly 4 times. `b_coord`: every row names a distinct block of dense_b. A block (K, J) belongs to the devices of grid column J // 14 and every grid row r with (r + J // 14) mod 4 = K // 8; among the 52 rows of one device, at most 4 name blocks of the same device, and every device that is named at all is named exactly 4 times.
All inputs are finite; a program needn't handle non-finite values. No bound on the sum of `c_keep` on one device may be relied on, other than what follows from the above.
Results may differ from a plain program's by a relative error of at most 0.001.
Values may be sent and summed in bfloat16 or wider, within the bound.
A program may use at most 192 MiB of HBM per device.

v0:
```python
import jax
import jax.numpy as jnp
from jax import lax
from jax.sharding import PartitionSpec as P

KB = 8
STEPS = 4


def from_behind(value, axis, steps):
    count = lax.axis_size(axis)
    pairs = [(source, (source + steps) % count) for source in range(count)]
    return lax.ppermute(value, axis, pairs)


def slot_targets(owners, devices, capacity):
    matches = (owners[:, None] == jnp.arange(devices, dtype=jnp.int32)[None, :]).astype(jnp.int32)
    order_rank = jnp.sum((jnp.cumsum(matches, axis=0) - 1) * matches, axis=1)
    return owners * capacity + order_rank


def as_slots(values, slot_count, trailing):
    return values.reshape((slot_count,) + trailing)


def on_device(a_blocks, a_coord, b_blocks, b_coord, c_keep):
    n_rows = lax.axis_size("row")
    n_cols = lax.axis_size("col")
    devices = n_rows * n_cols
    copies = n_rows // n_cols
    capacity = max(2, 128 // devices)
    slot_count = devices * capacity
    edge_size = a_blocks.shape[1]
    block_rows, block_cols = c_keep.shape
    a_grid_row = a_coord[:, 0] // block_rows
    a_part = a_coord[:, 1] // KB
    a_owner = a_grid_row * n_cols + (a_part - a_grid_row) % n_cols
    a_target = slot_targets(a_owner, devices, capacity)
    b_part = b_coord[:, 0] // KB
    b_grid_col = b_coord[:, 1] // block_cols
    b_first = (b_part - b_grid_col) % n_cols
    copy_rows = b_first[:, None] + n_cols * jnp.arange(copies, dtype=jnp.int32)[None, :]
    b_owner = (copy_rows * n_cols + b_grid_col[:, None]).reshape(-1)
    b_target = slot_targets(b_owner, devices, capacity)
    b_source = jnp.repeat(jnp.arange(b_blocks.shape[0], dtype=jnp.int32), copies)
    a_send = jnp.zeros((slot_count, edge_size, edge_size), jnp.bfloat16).at[a_target].set(a_blocks)
    a_where = jnp.full((slot_count, 2), -1, jnp.int32).at[a_target].set(a_coord)
    b_send = (
        jnp.zeros((slot_count, edge_size, edge_size), jnp.bfloat16)
        .at[b_target]
        .set(b_blocks[b_source])
    )
    b_where = jnp.full((slot_count, 2), -1, jnp.int32).at[b_target].set(b_coord[b_source])

    def flat_shape(values):
        return values.reshape((devices, capacity) + values.shape[1:])

    arrived = (
        lax.all_to_all(flat_shape(a_send), ("row", "col"), split_axis=0, concat_axis=0, tiled=True),
        lax.all_to_all(flat_shape(b_send), ("row", "col"), split_axis=0, concat_axis=0, tiled=True),
        lax.all_to_all(
            flat_shape(a_where), ("row", "col"), split_axis=0, concat_axis=0, tiled=True
        ),
        lax.all_to_all(
            flat_shape(b_where), ("row", "col"), split_axis=0, concat_axis=0, tiled=True
        ),
    )
    a_recv = as_slots(arrived[0], slot_count, (edge_size, edge_size))
    b_recv = as_slots(arrived[1], slot_count, (edge_size, edge_size))
    a_from = as_slots(arrived[2], slot_count, (2,))
    b_from = as_slots(arrived[3], slot_count, (2,))
    a_valid = a_from[:, 0] >= 0
    a_slot_row = jnp.where(a_valid, a_from[:, 0] % block_rows, block_rows)
    a_slot_col = a_from[:, 1] % KB
    a_panel = (
        jnp.zeros((block_rows, edge_size, KB, edge_size), jnp.bfloat16)
        .at[a_slot_row, :, a_slot_col, :]
        .set(a_recv, mode="drop")
    )
    a_matrix = a_panel.reshape(block_rows * edge_size, KB * edge_size)
    b_valid = b_from[:, 0] >= 0
    b_slot_row = jnp.where(b_valid, b_from[:, 0] % KB, KB)
    b_slot_col = b_from[:, 1] % block_cols
    b_panel = (
        jnp.zeros((KB, edge_size, block_cols, edge_size), jnp.bfloat16)
        .at[b_slot_row, :, b_slot_col, :]
        .set(b_recv, mode="drop")
    )
    b_matrix = b_panel.reshape(KB * edge_size, block_cols * edge_size)
    summed = jnp.zeros((block_rows * edge_size, block_cols * edge_size), jnp.float32)
    for step_index in range(STEPS):
        summed = summed + jnp.dot(a_matrix, b_matrix, preferred_element_type=jnp.float32)
        if step_index + 1 < STEPS:
            a_matrix = from_behind(a_matrix, "col", -1)
            b_matrix = from_behind(b_matrix, "row", -1)
    masked = (
        summed.reshape(block_rows, edge_size, block_cols, edge_size)
        * c_keep.astype(jnp.float32)[:, None, :, None]
    )
    return masked.reshape(block_rows * edge_size, block_cols * edge_size).astype(jnp.bfloat16)


def solution(mesh):
    return jax.shard_map(
        on_device,
        mesh=mesh,
        in_specs=(
            P(("row", "col"), None, None),
            P(("row", "col"), None),
            P(("row", "col"), None, None),
            P(("row", "col"), None),
            P("row", "col"),
        ),
        out_specs=P("row", "col"),
        check_vma=False,
    )
```

profile of v0, /device:TPU:0, one launch (start us, length us, event | category | flops | bytes accessed | tf_op | source)
XLA Modules:
  0.0 544.3 jit_solution(17211772551917615243)
XLA Ops:
  4.6 7.3 %all-to-all-start = ((s32[32,4,2]{1,2,0:T(2,128)}), s32[32,4,2]{1,2,0:T(2,128)S(1)}, u32[]{:S(2)}, u32[]{:S(2)}) async-start(s32[32,4,2]{1,2,0:T(2,128)} %copy.15), calls=%async_computation | async-start | bytes 65536 | tf_op jit(solution)/shard_map/all_to_all | solution.py:61
  19.2 3.1 all-to-all-start.2
  25.3 16.7 %scatter_fusion = bf16[128,128,128]{2,1,0:T(8,128)(2,1)} fusion(bf16[128,128,128]{2,1,0:T(8,128)(2,1)} %broadcast.231.clone, s32[104]{0:T(128)S(1)} %fusion.16, bf16[104,128,128]{2,1,0:T(8,128)(2,1)} %param.5), kind=kCustom, calls=%fused_computation.3 | custom fusion | bytes 10224032 | tf_op jit(solution)/shard_map/scatter | solution.py:46
  42.1 6.0 %all-to-all-start.1 = ((bf16[32,4,128,128]{3,2,1,0:T(8,128)(2,1)}), bf16[32,4,128,128]{3,2,1,0:T(8,128)(2,1)}, u32[]{:S(2)}, u32[]{:S(2)}) async-start(bf16[32,4,128,128]{3,2,1,0:T(8,128)(2,1)} %bitcast.67), calls=%async_computation.1 | async-start | bytes 8388608 | tf_op jit(solution)/shard_map/all_to_all | solution.py:59
  53.9 16.9 %scatter_fusion.2 = bf16[128,128,128]{2,1,0:T(8,128)(2,1)} fusion(bf16[128,128,128]{2,1,0:T(8,128)(2,1)} %broadcast.231.clone.1, s32[104]{0:T(128)S(1)} %fusion.17, bf16[104,128,128]{2,1,0:T(8,128)(2,1)} %gather_fusion), kind=kCustom, calls=%fused_computation.6 | custom fusion | bytes 10224032 | tf_op jit(solution)/shard_map/scatter | solution.py:51
  70.8 69.5 %all-to-all-done.1 = bf16[32,4,128,128]{3,2,1,0:T(8,128)(2,1)} async-done(((bf16[32,4,128,128]{3,2,1,0:T(8,128)(2,1)}), bf16[32,4,128,128]{3,2,1,0:T(8,128)(2,1)}, u32[]{:S(2)}, u32[]{:S(2)}) %all-to-all-start.1) | async-done | bytes 4194336 | tf_op jit(solution)/shard_map/all_to_all | solution.py:59
  140.3 5.7 %all-to-all-start.3 = ((bf16[32,4,128,128]{3,2,1,0:T(8,128)(2,1)}), bf16[32,4,128,128]{3,2,1,0:T(8,128)(2,1)}, u32[]{:S(2)}, u32[]{:S(2)}) async-start(bf16[32,4,128,128]{3,2,1,0:T(8,128)(2,1)} %bitcast.66), calls=%async_computation.3 | async-start | bytes 8388608 | tf_op jit(solution)/shard_map/all_to_all | solution.py:60
  149.0 20.6 %scatter_fusion.1 = bf16[14,128,8,128]{3,1,2,0:T(8,128)(2,1)} fusion(bf16[14,128,8,128]{3,1,2,0:T(8,128)(2,1)} %broadcast_in_dim.10, s32[128]{0:T(128)S(1)} %fusion.19, bf16[128,128,128]{2,1,0:T(8,128)(2,1)} %bitcast.6), kind=kCustom, calls=%fused_computation.4 | custom fusion | bytes 12583936 | tf_op jit(solution)/shard_map/scatter | solution.py:78
  169.7 5.0 copy.17
  177.7 3.5 collective-permute-start
  181.3 57.3 %all-to-all-done.3 = bf16[32,4,128,128]{3,2,1,0:T(8,128)(2,1)} async-done(((bf16[32,4,128,128]{3,2,1,0:T(8,128)(2,1)}), bf16[32,4,128,128]{3,2,1,0:T(8,128)(2,1)}, u32[]{:S(2)}, u32[]{:S(2)}) %all-to-all-start.3) | async-done | bytes 4194336 | tf_op jit(solution)/shard_map/all_to_all | solution.py:60
  241.3 20.7 %scatter_fusion.3 = bf16[8,128,14,128]{3,1,2,0:T(8,128)(2,1)} fusion(bf16[8,128,14,128]{3,1,2,0:T(8,128)(2,1)} %broadcast_in_dim.11, s32[128]{0:T(128)S(1)} %fusion.20, bf16[128,128,128]{2,1,0:T(8,128)(2,1)} %bitcast.15), kind=kCustom, calls=%fused_computation.7 | custom fusion | bytes 12583936 | tf_op jit(solution)/shard_map/scatter | solution.py:87
  262.0 6.2 %copy.22 = bf16[8,128,14,128]{1,0,3,2:T(8,128)(2,1)} copy(bf16[8,128,14,128]{3,1,2,0:T(8,128)(2,1)} %scatter_fusion.3) | data formatting | bytes 7340032 | tf_op jit(solution)/shard_map/scatter | solution.py:87
  268.2 3.2 copy.35
  274.2 22.3 %collective-permute-done = bf16[1792,1024]{1,0:T(8,128)(2,1)} collective-permute-done((bf16[1792,1024]{1,0:T(8,128)(2,1)}, bf16[1792,1024]{1,0:T(8,128)(2,1)}, u32[]{:S(2)}, u32[]{:S(2)}) %collective-permute-start) | collective-permute-done | bytes 3670048 | tf_op jit(solution)/shard_map/ppermute | solution.py:13
  296.5 56.1 %collective-permute-start.2 = (bf16[1792,1024]{1,0:T(8,128)(2,1)}, bf16[1792,1024]{1,0:T(8,128)(2,1)S(1)}, u32[]{:S(2)}, u32[]{:S(2)}) collective-permute-start(bf16[1792,1024]{1,0:T(8,128)(2,1)} %collective-permute-done), channel_id=1, source_target_pairs={{0,3},{1,0},{2,1},{3,2},{4,7},{5,4},{6,5},{7,6},{8,11},{9,8},{10,9... | collective-permute-start | bytes 11010056 | tf_op jit(solution)/shard_map/ppermute | solution.py:13
  353.6 9.4 %fusion.21 = f32[1792,1792]{1,0:T(8,128)} fusion(bf16[224,8,8,128]{3,2,1,0:T(8,128)(2,1)S(1)} %bitcast.69, bf16[224,8,8,128]{3,2,1,0:T(8,128)(2,1)S(1)} %bitcast.71), kind=kOutput, calls=%fused_computation.81 | convolution fusion | flops 6576668672 | bytes 20185088 | tf_op jit(solution)/shard_map/dot_general | solution.py:92
  363.0 68.1 %collective-permute-done.2 = bf16[1792,1024]{1,0:T(8,128)(2,1)S(1)} collective-permute-done((bf16[1792,1024]{1,0:T(8,128)(2,1)}, bf16[1792,1024]{1,0:T(8,128)(2,1)S(1)}, u32[]{:S(2)}, u32[]{:S(2)}) %collective-permute-start.2) | collective-permute-done | bytes 3670048 | tf_op jit(solution)/shard_map/ppermute | solution.py:13
  431.1 3.9 collective-permute-start.4
  436.5 11.2 %fusion.22 = f32[1792,1792]{1,0:T(8,128)} fusion(bf16[1792,1024]{1,0:T(8,128)(2,1)} %collective-permute-done, bf16[1024,1792]{0,1:T(8,128)(2,1)S(1)} %collective-permute-done.1), kind=kOutput, calls=%fused_computation.82 | convolution fusion | flops 6576668672 | bytes 20185088 | tf_op jit(solution)/shard_map/dot_general | solution.py:92
  447.7 9.3 %fusion.23 = f32[1792,1792]{1,0:T(8,128)} fusion(bf16[1792,1024]{1,0:T(8,128)(2,1)S(1)} %collective-permute-done.2, bf16[1024,1792]{0,1:T(8,128)(2,1)S(1)} %collective-permute-done.3), kind=kOutput, calls=%fused_computation.83 | convolution fusion | flops 6576668672 | bytes 20185088 | tf_op jit(solution)/shard_map/dot_general | solution.py:92
  457.0 56.0 %collective-permute-done.4 = bf16[1792,1024]{1,0:T(8,128)(2,1)} collective-permute-done((bf16[1792,1024]{1,0:T(8,128)(2,1)S(1)}, bf16[1792,1024]{1,0:T(8,128)(2,1)}, u32[]{:S(2)}, u32[]{:S(2)}) %collective-permute-start.4) | collective-permute-done | bytes 3670048 | tf_op jit(solution)/shard_map/ppermute | solution.py:13
  513.0 6.2 %mul.72 = f32[14,128,14,128]{3,2,1,0:T(8,128)} broadcast(f32[14,14]{1,0:T(8,128)S(1)} %convert_element_type.14), dimensions={0,2} | broadcast | bytes 12845840 | tf_op jit(solution)/shard_map/mul | solution.py:97
  519.2 25.1 %fusion = bf16[1792,1792]{1,0:T(8,128)(2,1)} fusion(f32[224,8,14,128]{3,2,1,0:T(8,128)} %bitcast.65, f32[1792,1792]{1,0:T(8,128)} %fusion.23, f32[1792,1792]{1,0:T(8,128)} %fusion.21, f32[1792,1792]{1,0:T(8,128)} %fusion.22, bf16[1792,1024]{1,0:T(8,128)(2,1)} %collective-permute-done.4, bf16[1024,1792]{0,1:T(8,128)(2,1)} %collective-permute-done.5), kind=kOutput, calls=%fused_computation.9 | convolution fusion | flops 6592724992 | bytes 65142784 | tf_op jit(solution)/shard_map/dot_general | solution.py:92
  (57 shorter events, 34.7 us)
Async XLA Ops:
  0.0 48.1 %copy-start = (bf16[52,128,128]{2,1,0:T(8,128)(2,1)S(1)}, bf16[52,128,128]{2,1,0:T(8,128)(2,1)}, u32[]{:S(2)}) copy-start(bf16[52,128,128]{2,1,0:T(8,128)(2,1)} %param.7) | copy-start | bytes 5111812
  4.6 14.6 %all-to-all-start = ((s32[32,4,2]{1,2,0:T(2,128)}), s32[32,4,2]{1,2,0:T(2,128)S(1)}, u32[]{:S(2)}, u32[]{:S(2)}) async-start(s32[32,4,2]{1,2,0:T(2,128)} %copy.15), calls=%async_computation | async-start | bytes 65536 | tf_op jit(solution)/shard_map/all_to_all | solution.py:61
  19.2 22.9 %all-to-all-start.2 = ((s32[32,4,2]{1,2,0:T(2,128)}), s32[32,4,2]{1,2,0:T(2,128)S(1)}, u32[]{:S(2)}, u32[]{:S(2)}) async-start(s32[32,4,2]{1,2,0:T(2,128)} %copy.20), calls=%async_computation.2 | async-start | bytes 65536 | tf_op jit(solution)/shard_map/all_to_all | solution.py:64
  42.1 98.2 %all-to-all-start.1 = ((bf16[32,4,128,128]{3,2,1,0:T(8,128)(2,1)}), bf16[32,4,128,128]{3,2,1,0:T(8,128)(2,1)}, u32[]{:S(2)}, u32[]{:S(2)}) async-start(bf16[32,4,128,128]{3,2,1,0:T(8,128)(2,1)} %bitcast.67), calls=%async_computation.1 | async-start | bytes 8388608 | tf_op jit(solution)/shard_map/all_to_all | solution.py:59
  140.3 98.3 %all-to-all-start.3 = ((bf16[32,4,128,128]{3,2,1,0:T(8,128)(2,1)}), bf16[32,4,128,128]{3,2,1,0:T(8,128)(2,1)}, u32[]{:S(2)}, u32[]{:S(2)}) async-start(bf16[32,4,128,128]{3,2,1,0:T(8,128)(2,1)} %bitcast.66), calls=%async_computation.3 | async-start | bytes 8388608 | tf_op jit(solution)/shard_map/all_to_all | solution.py:60
  174.7 3.0 copy-start.2
  177.7 118.7 %collective-permute-start = (bf16[1792,1024]{1,0:T(8,128)(2,1)}, bf16[1792,1024]{1,0:T(8,128)(2,1)}, u32[]{:S(2)}, u32[]{:S(2)}) collective-permute-start(bf16[1792,1024]{1,0:T(8,128)(2,1)} %bitcast.58), channel_id=1, source_target_pairs={{0,3},{1,0},{2,1},{3,2},{4,7},{5,4},{6,5},{7,6},{8,11},{9,8},{10,9... | collective-permute-start | bytes 11010056 | tf_op jit(solution)/shard_map/ppermute | solution.py:13
  262.0 91.6 %copy-start.5 = (s32[14,14]{1,0:T(8,128)S(1)}, s32[14,14]{1,0:T(8,128)}, u32[]{:S(2)}) copy-start(s32[14,14]{1,0:T(8,128)} %param.9) | copy-start | bytes 2356
  268.2 85.4 %copy-start.3 = (bf16[14,128,8,128]{3,2,1,0:T(8,128)(2,1)S(1)}, bf16[14,128,8,128]{3,2,1,0:T(8,128)(2,1)}, u32[]{:S(2)}) copy-start(bf16[14,128,8,128]{3,2,1,0:T(8,128)(2,1)} %copy-done.2) | copy-start | bytes 11010052
  268.2 85.4 %copy-start.4 = (bf16[8,128,14,128]{1,0,3,2:T(8,128)(2,1)S(1)}, bf16[8,128,14,128]{1,0,3,2:T(8,128)(2,1)}, u32[]{:S(2)}) copy-start(bf16[8,128,14,128]{1,0,3,2:T(8,128)(2,1)} %copy.22) | copy-start | bytes 11010052
  271.4 81.1 %collective-permute-start.1 = (bf16[1024,1792]{0,1:T(8,128)(2,1)S(1)}, bf16[1024,1792]{0,1:T(8,128)(2,1)S(1)}, u32[]{:S(2)}, u32[]{:S(2)}) collective-permute-start(bf16[1024,1792]{0,1:T(8,128)(2,1)S(1)} %bitcast.72), channel_id=1, source_target_pairs={{0,28},{4,0},{8,4},{12,8},{16,12},{20,16},{24,20},{28,24},{1,29},{... | collective-permute-start | bytes 11010056 | tf_op jit(solution)/shard_map/ppermute | solution.py:13
  296.5 134.7 %collective-permute-start.2 = (bf16[1792,1024]{1,0:T(8,128)(2,1)}, bf16[1792,1024]{1,0:T(8,128)(2,1)S(1)}, u32[]{:S(2)}, u32[]{:S(2)}) collective-permute-start(bf16[1792,1024]{1,0:T(8,128)(2,1)} %collective-permute-done), channel_id=1, source_target_pairs={{0,3},{1,0},{2,1},{3,2},{4,7},{5,4},{6,5},{7,6},{8,11},{9,8},{10,9... | collective-permute-start | bytes 11010056 | tf_op jit(solution)/shard_map/ppermute | solution.py:13
  352.6 82.5 %collective-permute-start.3 = (bf16[1024,1792]{0,1:T(8,128)(2,1)S(1)}, bf16[1024,1792]{0,1:T(8,128)(2,1)S(1)}, u32[]{:S(2)}, u32[]{:S(2)}) collective-permute-start(bf16[1024,1792]{0,1:T(8,128)(2,1)S(1)} %collective-permute-done.1), channel_id=1, source_target_pairs={{0,28},{4,0},{8,4},{12,8},{16,12},{20,16},{24,20},{28,24},{1,29},{... | collective-permute-start | bytes 11010056 | tf_op jit(solution)/shard_map/ppermute | solution.py:13
  431.1 81.8 %collective-permute-start.4 = (bf16[1792,1024]{1,0:T(8,128)(2,1)S(1)}, bf16[1792,1024]{1,0:T(8,128)(2,1)}, u32[]{:S(2)}, u32[]{:S(2)}) collective-permute-start(bf16[1792,1024]{1,0:T(8,128)(2,1)S(1)} %collective-permute-done.2), channel_id=1, source_target_pairs={{0,3},{1,0},{2,1},{3,2},{4,7},{5,4},{6,5},{7,6},{8,11},{9,8},{10,9... | collective-permute-start | bytes 11010056 | tf_op jit(solution)/shard_map/ppermute | solution.py:13
  435.1 77.9 %collective-permute-start.5 = (bf16[1024,1792]{0,1:T(8,128)(2,1)S(1)}, bf16[1024,1792]{0,1:T(8,128)(2,1)}, u32[]{:S(2)}, u32[]{:S(2)}) collective-permute-start(bf16[1024,1792]{0,1:T(8,128)(2,1)S(1)} %collective-permute-done.3), channel_id=1, source_target_pairs={{0,28},{4,0},{8,4},{12,8},{16,12},{20,16},{24,20},{28,24},{1,29},{... | collective-permute-start | bytes 11010056 | tf_op jit(solution)/shard_map/ppermute | solution.py:13
  519.2 25.1 %copy-start.1 = (bf16[52,128,128]{2,1,0:T(8,128)(2,1)S(1)}, bf16[52,128,128]{2,1,0:T(8,128)(2,1)}, u32[]{:S(2)}) copy-start(bf16[52,128,128]{2,1,0:T(8,128)(2,1)} %param.7) | copy-start | bytes 5111812
where the time goes:
time: 546 us; the launch traced here: 544 us
  waiting for transfers between devices  276 us (51%)
  local copies, waits for them, and re-layouts  119 us (22%)
  starting transfers between devices  90.8 us (17%)
  matrix products  55 us (10%)
    ppermute x6, waiting for transfers between devices, from_behind(): return lax.ppermute(value, axis, pairs)  146 us
    all_to_all x1, waiting for transfers between devices, on_device(): lax.all_to_all(flat_shape(a_send), ('row', 'col'), split_axis=0, concat_a...  69.5 us
    ppermute x6, starting transfers between devices, from_behind(): return lax.ppermute(value, axis, pairs)  68.8 us
    all_to_all x1, waiting for transfers between devices, on_device(): lax.all_to_all(flat_shape(b_send), ('row', 'col'), split_axis=0, concat_a...  57.3 us
    dot_general x4, matrix products, on_device(): jnp.dot(a_matrix, b_matrix, preferred_element_type=jnp.float32)  55 us
    scatter x2, local copies, waits for them, and re-layouts, on_device(): b_panel = jnp.zeros((KB, edge_size, block_cols, edge_size), jnp.bfloat16)...  26.9 us
    scatter x2, local copies, waits for them, and re-layouts, on_device(): a_panel = jnp.zeros((block_rows, edge_size, KB, edge_size), jnp.bfloat16)...  25.7 us
    scatter x1, local copies, waits for them, and re-layouts, on_device(): b_send = jnp.zeros((slot_count, edge_size, edge_size), jnp.bfloat16).at[b...  16.9 us
  transfers between devices with their start and end apart: 10, of which 6 were waited for; matrix products, arithmetic and copies ran while one was open for 26% of the time, Pallas kernels for 0%

commit v1 on v0

--- a/solution.py
+++ b/solution.py
@@ -1,10 +1,15 @@
+import functools
+
 import jax
 import jax.numpy as jnp
 from jax import lax
+from jax.experimental import pallas as pl
+from jax.experimental.pallas import tpu as pltpu
 from jax.sharding import PartitionSpec as P
 
 KB = 8
 STEPS = 4
+MESH = pl.DeviceIdType.MESH
 
 
 def from_behind(value, axis, steps):
@@ -23,7 +28,7 @@
     return values.reshape((slot_count,) + trailing)
 
 
-def on_device(a_blocks, a_coord, b_blocks, b_coord, c_keep):
+def stepwise(a_blocks, a_coord, b_blocks, b_coord, c_keep):
     n_rows = lax.axis_size("row")
     n_cols = lax.axis_size("col")
     devices = n_rows * n_cols
@@ -52,38 +57,26 @@
     )
     b_where = jnp.full((slot_count, 2), -1, jnp.int32).at[b_target].set(b_coord[b_source])
 
-    def flat_shape(values):
-        return values.reshape((devices, capacity) + values.shape[1:])
-
-    arrived = (
-        lax.all_to_all(flat_shape(a_send), ("row", "col"), split_axis=0, concat_axis=0, tiled=True),
-        lax.all_to_all(flat_shape(b_send), ("row", "col"), split_axis=0, concat_axis=0, tiled=True),
-        lax.all_to_all(
-            flat_shape(a_where), ("row", "col"), split_axis=0, concat_axis=0, tiled=True
-        ),
-        lax.all_to_all(
-            flat_shape(b_where), ("row", "col"), split_axis=0, concat_axis=0, tiled=True
-        ),
-    )
-    a_recv = as_slots(arrived[0], slot_count, (edge_size, edge_size))
-    b_recv = as_slots(arrived[1], slot_count, (edge_size, edge_size))
-    a_from = as_slots(arrived[2], slot_count, (2,))
-    b_from = as_slots(arrived[3], slot_count, (2,))
-    a_valid = a_from[:, 0] >= 0
-    a_slot_row = jnp.where(a_valid, a_from[:, 0] % block_rows, block_rows)
-    a_slot_col = a_from[:, 1] % KB
+    def exchange(values, trailing):
+        shaped = values.reshape((devices, capacity) + values.shape[1:])
+        got = lax.all_to_all(shaped, ("row", "col"), split_axis=0, concat_axis=0, tiled=True)
+        return as_slots(got, slot_count, trailing)
+
+    a_recv = exchange(a_send, (edge_size, edge_size))
+    b_recv = exchange(b_send, (edge_size, edge_size))
+    a_from = exchange(a_where, (2,))
+    b_from = exchange(b_where, (2,))
+    a_slot_row = jnp.where(a_from[:, 0] >= 0, a_from[:, 0] % block_rows, block_rows)
     a_panel = (
         jnp.zeros((block_rows, edge_size, KB, edge_size), jnp.bfloat16)
-        .at[a_slot_row, :, a_slot_col, :]
+        .at[a_slot_row, :, a_from[:, 1] % KB, :]
         .set(a_recv, mode="drop")
     )
     a_matrix = a_panel.reshape(block_rows * edge_size, KB * edge_size)
-    b_valid = b_from[:, 0] >= 0
-    b_slot_row = jnp.where(b_valid, b_from[:, 0] % KB, KB)
-    b_slot_col = b_from[:, 1] % block_cols
+    b_slot_row = jnp.where(b_from[:, 0] >= 0, b_from[:, 0] % KB, KB)
     b_panel = (
         jnp.zeros((KB, edge_size, block_cols, edge_size), jnp.bfloat16)
-        .at[b_slot_row, :, b_slot_col, :]
+        .at[b_slot_row, :, b_from[:, 1] % block_cols, :]
         .set(b_recv, mode="drop")
     )
     b_matrix = b_panel.reshape(KB * edge_size, block_cols * edge_size)
@@ -100,9 +93,287 @@
     return masked.reshape(block_rows * edge_size, block_cols * edge_size).astype(jnp.bfloat16)
 
 
+def fused_kernel(
+    n_rows, n_cols, cap, rb, cb, bs,
+    a_index, b_index, a_send, b_send, keep, out,
+    a_parts, b_parts, a_dense, b_dense, acc, stage,
+    ax_send, ax_recv, bz_send, bz_recv, bx_send, bx_recv, az_send, az_recv, own_sem, out_sem,
+):
+    r = lax.axis_index("row")
+    z = lax.axis_index("col")
+    plane = n_rows * cap
+    line = n_cols * cap
+    zero_slot = n_rows * n_cols * cap
+
+    barrier = pltpu.get_barrier_semaphore()
+    for d in range(1, n_rows):
+        pl.semaphore_signal(barrier, inc=1, device_id=(lax.rem(r + d, n_rows), z), device_id_type=MESH)
+    for d in range(1, n_cols):
+        pl.semaphore_signal(barrier, inc=1, device_id=(r, lax.rem(z + d, n_cols)), device_id_type=MESH)
+    pl.semaphore_wait(barrier, n_rows + n_cols - 2)
+
+    def ax(p, d):
+        to = lax.rem(r + d, n_rows)
+        return pltpu.make_async_remote_copy(
+            src_ref=a_send.at[p, to],
+            dst_ref=a_parts[p].at[pl.ds(z * plane + r * cap, cap)],
+            send_sem=ax_send.at[p, d - 1],
+            recv_sem=ax_recv.at[p, d - 1],
+            device_id=(to, z),
+            device_id_type=MESH,
+        )
+
+    def ax_own(p):
+        return pltpu.make_async_copy(
+            a_send.at[p, r], a_parts[p].at[pl.ds(z * plane + r * cap, cap)], own_sem.at[0, p]
+        )
+
+    def bz(p, d):
+        to = lax.rem(z + d, n_cols)
+        return pltpu.make_async_remote_copy(
+            src_ref=b_send.at[p, to],
+            dst_ref=b_parts[p].at[pl.ds(r * line + z * cap, cap)],
+            send_sem=bz_send.at[p, d - 1],
+            recv_sem=bz_recv.at[p, d - 1],
+            device_id=(r, to),
+            device_id_type=MESH,
+        )
+
+    def bz_own(p):
+        return pltpu.make_async_copy(
+            b_send.at[p, z], b_parts[p].at[pl.ds(r * line + z * cap, cap)], own_sem.at[1, p]
+        )
+
+    def bx(p, d):
+        section = b_parts[p].at[pl.ds(r * line, line)]
+        return pltpu.make_async_remote_copy(
+            src_ref=section,
+            dst_ref=section,
+            send_sem=bx_send.at[p, d - 1],
+            recv_sem=bx_recv.at[p, d - 1],
+            device_id=(lax.rem(r + d, n_rows), z),
+            device_id_type=MESH,
+        )
+
+    def az(p, hop, way):
+        origin = z - hop * way
+        section = a_parts[p].at[pl.ds(origin * plane, plane)]
+        return pltpu.make_async_remote_copy(
+            src_ref=section,
+            dst_ref=section,
+            send_sem=az_send.at[p, hop, (way + 1) // 2],
+            recv_sem=az_recv.at[p, hop, (way + 1) // 2],
+            device_id=(r, z + way),
+            device_id_type=MESH,
+        )
+
+    def arrived(p, hop, way):
+        section = a_parts[p].at[pl.ds((z - hop * way) * plane, plane)]
+        return pltpu.make_async_remote_copy(
+            src_ref=section,
+            dst_ref=section,
+            send_sem=az_send.at[p, hop - 1, (way + 1) // 2],
+            recv_sem=az_recv.at[p, hop - 1, (way + 1) // 2],
+            device_id=(r, z - way),
+            device_id_type=MESH,
+        )
+
+    def can_send(hop, way):
+        if way == 1:
+            return jnp.logical_and(z >= hop, z < n_cols - 1)
+        return jnp.logical_and(z + hop < n_cols, z > 0)
+
+    def can_receive(hop, way):
+        return z >= hop if way == 1 else z + hop < n_cols
+
+    def open_part(p):
+        for d in range(1, n_rows):
+            ax(p, d).wait_recv()
+        ax_own(p).wait()
+        for way in (1, -1):
+            @pl.when(can_send(0, way))
+            def _():
+                az(p, 0, way).start()
+        for d in range(1, n_cols):
+            bz(p, d).wait_recv()
+        bz_own(p).wait()
+        for d in range(1, n_rows):
+            bx(p, d).start()
+
+    def relay(p):
+        for hop in range(1, n_cols):
+            for way in (1, -1):
+                @pl.when(can_receive(hop, way))
+                def _():
+                    arrived(p, hop, way).wait_recv()
+                if hop < n_cols - 1:
+                    @pl.when(can_send(hop, way))
+                    def _():
+                        az(p, hop, way).start()
+
+    def multiply(p):
+        for d in range(1, n_rows):
+            bx(p, d).wait_recv()
+
+        def place_a(i, carry):
+            rows = pl.ds(pl.multiple_of(i * bs, bs), bs)
+            for k in range(KB):
+                a_dense[rows, k * bs:(k + 1) * bs] = a_parts[p][a_index[p, i * KB + k]]
+            return carry
+
+        lax.fori_loop(0, rb, place_a, 0)
+
+        def place_b(k, carry):
+            rows = pl.ds(pl.multiple_of(k * bs, bs), bs)
+            for j in range(cb):
+                b_dense[rows, j * bs:(j + 1) * bs] = b_parts[p][b_index[p, k * cb + j]]
+            return carry
+
+        lax.fori_loop(0, KB, place_b, 0)
+
+        wide = 2 * bs
+        tall = rb * bs // 2
+
+        def tile(t, carry):
+            rows = pl.ds(pl.multiple_of((t % 2) * tall, tall), tall)
+            cols = pl.ds(pl.multiple_of((t // 2) * wide, wide), wide)
+            term = jnp.dot(a_dense[rows, :], b_dense[:, cols], preferred_element_type=jnp.float32)
+            acc[rows, cols] = term if p == 0 else acc[rows, cols] + term
+            return carry
+
+        lax.fori_loop(0, 2 * (cb * bs // wide), tile, 0)
+
+    for p in range(n_cols):
+        for d in range(1, n_rows):
+            ax(p, d).start()
+        ax_own(p).start()
+        for d in range(1, n_cols):
+            bz(p, d).start()
+        bz_own(p).start()
+    for p in range(n_cols):
+        a_parts[p][zero_slot] = jnp.zeros((bs, bs), jnp.bfloat16)
+        b_parts[p][zero_slot] = jnp.zeros((bs, bs), jnp.bfloat16)
+
+    open_part(0)
+    for p in range(n_cols):
+        if p + 1 < n_cols:
+            open_part(p + 1)
+        relay(p)
+        multiply(p)
+
+    def finish(i):
+        return pltpu.make_async_copy(
+            stage.at[i * bs:(i + 1) * bs], out.at[i * bs:(i + 1) * bs], out_sem.at[i]
+        )
+
+    for i in range(rb):
+        rows = slice(i * bs, (i + 1) * bs)
+        stage[rows, :] = (acc[rows, :] * keep[i:i + 1, :]).astype(jnp.bfloat16)
+        finish(i).start()
+    for p in range(n_cols):
+        for d in range(1, n_rows):
+            ax(p, d).wait_send()
+            bx(p, d).wait_send()
+        for d in range(1, n_cols):
+            bz(p, d).wait_send()
+        for hop in range(n_cols - 1):
+            for way in (1, -1):
+                @pl.when(can_send(hop, way))
+                def _():
+                    az(p, hop, way).wait_send()
+    for i in range(rb):
+        finish(i).wait()
+
+
+def slot_sources(owner, count, cap):
+    same = owner[:, None] == owner[None, :]
+    total = owner.shape[0]
+    earlier = jnp.arange(total)[None, :] < jnp.arange(total)[:, None]
+    rank = jnp.sum((same & earlier).astype(jnp.int32), axis=1)
+    target = owner * cap + rank
+    hit = target[:, None] == jnp.arange(count * cap, dtype=jnp.int32)[None, :]
+    order = jnp.arange(total, dtype=jnp.int32)[:, None]
+    return jnp.max(jnp.where(hit, order, -1), axis=0), hit
+
+
+def gathered(a_blocks, a_coord, b_blocks, b_coord, c_keep):
+    n_rows = lax.axis_size("row")
+    n_cols = lax.axis_size("col")
+    devices = n_rows * n_cols
+    cap = max(2, 128 // devices)
+    bs = a_blocks.shape[1]
+    rb, cb = c_keep.shape
+    a_owner = (a_coord[:, 1] // KB) * n_rows + a_coord[:, 0] // rb
+    b_owner = (b_coord[:, 0] // KB) * n_cols + b_coord[:, 1] // cb
+    a_source, a_hit = slot_sources(a_owner, devices, cap)
+    b_source, b_hit = slot_sources(b_owner, n_cols * n_cols, cap)
+    a_place = (a_coord[:, 0] % rb) * KB + a_coord[:, 1] % KB
+    b_place = (b_coord[:, 0] % KB) * cb + b_coord[:, 1] % cb
+    a_slot = jnp.max(jnp.where(a_hit, a_place[:, None], -1), axis=0)
+    b_slot = jnp.max(jnp.where(b_hit, b_place[:, None], -1), axis=0)
+    a_send = jnp.take(a_blocks, jnp.maximum(a_source, 0), axis=0, mode="clip")
+    b_send = jnp.take(b_blocks, jnp.maximum(b_source, 0), axis=0, mode="clip")
+    a_send = a_send.reshape(n_cols, n_rows, cap, bs, bs)
+    b_send = b_send.reshape(n_cols, n_cols, cap, bs, bs)
+
+    slots = lax.all_gather(jnp.concatenate([a_slot, b_slot]), ("row", "col"))
+    r = lax.axis_index("row")
+    z = lax.axis_index("col")
+    a_all = slots[:, : devices * cap].reshape(n_rows, n_cols, n_cols, n_rows, cap)
+    a_mine = lax.dynamic_index_in_dim(a_all, r, 3, keepdims=False)
+    a_mine = a_mine.transpose(2, 1, 0, 3).reshape(n_cols, devices * cap)
+    b_all = slots[:, devices * cap:].reshape(n_rows, n_cols, n_cols, n_cols, cap)
+    b_mine = lax.dynamic_index_in_dim(b_all, z, 3, keepdims=False)
+    b_mine = b_mine.transpose(2, 0, 1, 3).reshape(n_cols, devices * cap)
+
+    def invert(mine, places):
+        hit = mine[:, :, None] == jnp.arange(places, dtype=jnp.int32)[None, None, :]
+        order = jnp.arange(devices * cap, dtype=jnp.int32)[None, :, None]
+        return jnp.min(jnp.where(hit, order, devices * cap), axis=1)
+
+    keep = jnp.repeat(c_keep.astype(jnp.float32), bs, axis=1)
+    held = devices * cap + 1
+    part = pltpu.VMEM((held, bs, bs), jnp.bfloat16)
+    dma = pltpu.SemaphoreType.DMA
+    return pl.pallas_call(
+        functools.partial(fused_kernel, n_rows, n_cols, cap, rb, cb, bs),
+        out_shape=jax.ShapeDtypeStruct((rb * bs, cb * bs), jnp.bfloat16),
+        in_specs=[
+            pl.BlockSpec(memory_space=pltpu.SMEM),
+            pl.BlockSpec(memory_space=pltpu.SMEM),
+            pl.BlockSpec(memory_space=pl.ANY),
+            pl.BlockSpec(memory_space=pl.ANY),
+            pl.BlockSpec(memory_space=pltpu.VMEM),
+        ],
+        out_specs=pl.BlockSpec(memory_space=pl.ANY),
+        scratch_shapes=[
+            [part] * n_cols,
+            [part] * n_cols,
+            pltpu.VMEM((rb * bs, KB * bs), jnp.bfloat16),
+            pltpu.VMEM((KB * bs, cb * bs), jnp.bfloat16),
+            pltpu.VMEM((rb * bs, cb * bs), jnp.float32),
+            pltpu.VMEM((rb * bs, cb * bs), jnp.bfloat16),
+            dma((n_cols, n_rows - 1)),
+            dma((n_cols, n_rows - 1)),
+            dma((n_cols, n_cols - 1)),
+            dma((n_cols, n_cols - 1)),
+            dma((n_cols, n_rows - 1)),
+            dma((n_cols, n_rows - 1)),
+            dma((n_cols, n_cols - 1, 2)),
+            dma((n_cols, n_cols - 1, 2)),
+            dma((2, n_cols)),
+            dma((rb,)),
+        ],
+        compiler_params=pltpu.CompilerParams(
+            collective_id=0, has_side_effects=True, vmem_limit_bytes=60 * 2**20
+        ),
+    )(invert(a_mine, rb * KB), invert(b_mine, KB * cb), a_send, b_send, keep)
+
+
 def solution(mesh):
+    whole_window = mesh.shape["col"] == STEPS
     return jax.shard_map(
-        on_device,
+        gathered if whole_window else stepwise,
         mesh=mesh,
         in_specs=(
             P(("row", "col"), None, None),

time: 546 us -> 406 us (0.74)
  Pallas kernels: 0 us -> 339 us
  waiting for transfers between devices: 276 us -> 0 us
  local copies, waits for them, and re-layouts: 119 us -> 18.6 us
  starting transfers between devices: 90.8 us -> 0 us
  matrix products: 55 us -> 0 us
  blocking collectives: 0 us -> 42.2 us
    pallas_call x0 -> x1, Pallas kernels: none -> 339 us  [gathered(): pl.pallas_call(functools.partial(fused_kernel, n_rows, n_cols, cap, rb, c...]
    ppermute x6 -> x0, waiting for transfers between devices: 146 us -> none  [from_behind(): return lax.ppermute(value, axis, pairs)]
    all_to_all x4 -> x0, waiting for transfers between devices: 130 us -> none  [the longest x1 69.5 us: on_device(): lax.all_to_all(flat_shape(a_send), ('row', 'col'), split_axis=0, concat_a...]
    scatter x8 -> x0, local copies, waits for them, and re-layouts: 88.1 us -> none  [the longest x2 26.9 us: on_device(): b_panel = jnp.zeros((KB, edge_size, block_cols, edge_size), jnp.bfloat16)...]
    ppermute x6 -> x0, starting transfers between devices: 68.8 us -> none  [from_behind(): return lax.ppermute(value, axis, pairs)]
    dot_general x4 -> x0, matrix products: 55 us -> none  [on_device(): jnp.dot(a_matrix, b_matrix, preferred_element_type=jnp.float32)]
    unnamed x0 -> x1, blocking collectives: none -> 42.2 us
    all_to_all x4 -> x0, starting transfers between devices: 22 us -> none  [the longest x1 7.3 us: on_device(): lax.all_to_all(flat_shape(a_where), ('row', 'col'), split_axis=0, concat_...]
  transfers between devices with their start and end apart: 10 -> 0, of which waited for: 6 -> 0; matrix products, arithmetic and copies ran while one was open for 26% -> 0% of each run, Pallas kernels for 0% -> 0%
where the time goes in v1:
time: 406 us; the launch traced here: 405 us
  Pallas kernels  339 us (83%)
  blocking collectives  42.2 us (10%)
  local copies, waits for them, and re-layouts  18.6 us (5%)
  other arithmetic  5.52 us (1%)
    pallas_call x1, Pallas kernels, gathered(): pl.pallas_call(functools.partial(fused_kernel, n_rows, n_cols, cap, rb, c...  339 us
    unnamed x1, blocking collectives  42.2 us

profile of v1, /device:TPU:0, one launch (start us, length us, event | category | flops | bytes accessed | tf_op | source)
XLA Modules:
  0.0 405.0 jit_solution(2491063252975451342)
XLA Ops:
  0.0 0.9 fusion.4
  0.9 0.9 fusion.8
  1.8 0.2 convert_reduce_fusion
  2.0 0.1 select_reduce_fusion.2
  2.1 0.8 fusion.5
  2.9 0.8 fusion.9
  3.6 0.2 convert_reduce_fusion.1
  3.8 0.1 select_reduce_fusion.4
  4.0 0.7 convert_element_type.11
  4.8 42.2 %all-reduce = s32[6144]{0:T(1024)S(1)} all-reduce(s32[6144]{0:T(1024)S(1)} %add_dynamic-update-slice_fusion), channel_id=2, replica_groups=mesh['row'=8,'col'=4] {'row','col'}, use_global_device_ids=true, to_apply=%add | all-reduce | flops 6144 | bytes 49152
  47.1 0.7 copy.15
  47.8 1.0 reshape.154
  48.9 1.0 constant_dynamic-slice_fusion
  49.9 0.1 eq.116
  50.0 1.3 reshape.153
  51.4 1.1 constant_dynamic-slice_fusion.1
  52.4 0.2 copy.10
  52.6 0.2 copy.11
  52.8 0.1 eq.112
  52.9 0.8 select_reduce_fusion
  53.7 3.6 gather_fusion.1
  57.4 3.1 gather_fusion
  60.4 338.6 %shard_map.55 = bf16[1792,1792]{1,0:T(8,128)(2,1)} custom-call(s32[4,112]{1,0:T(4,128)} %get-tuple-element.16.a_index, s32[4,112]{1,0:T(4,128)} %get-tuple-element.15.b_index, bf16[4,8,4,128,128]{4,3,2,1,0:T(8,128)(2,1)} %bitcast.65, bf16[4,4,4,128,128]{4,3,2,1,0:T(8,128)(2,1)} %bitcast.66, f32[14,1792]{1,0:T(8,128)} %bitcast.68), custom_call_target="tpu_custom_call" | custom-call | tf_op jit(solution)/shard_map/pallas_call | solution.py:338
  399.1 6.0 %copy.20 = bf16[1792,1792]{1,0:T(8,128)(2,1)} copy(bf16[1792,1792]{1,0:T(8,128)(2,1)} %shard_map.55) | data formatting | bytes 12845056
  (16 shorter events, 0.3 us)
Async XLA Ops:
  0.0 57.3 %copy-start = (bf16[104,128,128]{2,1,0:T(8,128)(2,1)S(1)}, bf16[104,128,128]{2,1,0:T(8,128)(2,1)}, u32[]{:S(2)}) copy-start(bf16[104,128,128]{2,1,0:T(8,128)(2,1)} %param.5) | copy-start | bytes 10223620

commit v2 on v1

--- a/solution.py
+++ b/solution.py
@@ -316,15 +316,15 @@
     a_send = a_send.reshape(n_cols, n_rows, cap, bs, bs)
     b_send = b_send.reshape(n_cols, n_cols, cap, bs, bs)
 
-    slots = lax.all_gather(jnp.concatenate([a_slot, b_slot]), ("row", "col"))
-    r = lax.axis_index("row")
-    z = lax.axis_index("col")
-    a_all = slots[:, : devices * cap].reshape(n_rows, n_cols, n_cols, n_rows, cap)
-    a_mine = lax.dynamic_index_in_dim(a_all, r, 3, keepdims=False)
-    a_mine = a_mine.transpose(2, 1, 0, 3).reshape(n_cols, devices * cap)
-    b_all = slots[:, devices * cap:].reshape(n_rows, n_cols, n_cols, n_cols, cap)
-    b_mine = lax.dynamic_index_in_dim(b_all, z, 3, keepdims=False)
-    b_mine = b_mine.transpose(2, 0, 1, 3).reshape(n_cols, devices * cap)
+    a_to = a_slot.reshape(n_cols, n_rows, 1, cap).transpose(1, 2, 0, 3)
+    b_to = b_slot.reshape(n_cols, 1, n_cols, cap).transpose(1, 2, 0, 3)
+    shape = (n_rows, n_cols, n_cols, cap)
+    both = jnp.stack([jnp.broadcast_to(a_to, shape), jnp.broadcast_to(b_to, shape)], axis=2)
+    both = both.reshape(devices, 2 * n_cols * cap)
+    slots = lax.all_to_all(both, ("row", "col"), split_axis=0, concat_axis=0, tiled=True)
+    slots = slots.reshape(n_rows, n_cols, 2, n_cols, cap)
+    a_mine = slots[:, :, 0].transpose(2, 1, 0, 3).reshape(n_cols, devices * cap)
+    b_mine = slots[:, :, 1].transpose(2, 0, 1, 3).reshape(n_cols, devices * cap)
 
     def invert(mine, places):
         hit = mine[:, :, None] == jnp.arange(places, dtype=jnp.int32)[None, None, :]

time: 406 us -> 372 us (0.916)
  blocking collectives: 42.2 us -> 0 us
  starting transfers between devices: 0 us -> 7.3 us
    unnamed x1 -> x0, blocking collectives: 42.2 us -> none
    all_to_all x0 -> x1, starting transfers between devices: none -> 7.3 us  [gathered(): lax.all_to_all(both, ('row', 'col'), split_axis=0, concat_axis=0, tiled=T...]
  transfers between devices with their start and end apart: 0 -> 1, of which waited for: 0 -> 0; matrix products, arithmetic and copies ran while one was open for 0% -> 3% of each run, Pallas kernels for 0% -> 0%
where the time goes in v2:
time: 372 us
  Pallas kernels  339 us (91%)
  local copies, waits for them, and re-layouts  18.1 us (5%)
  other arithmetic  7.71 us (2%)
  starting transfers between devices  7.3 us (2%)
    pallas_call x1, Pallas kernels, gathered(): pl.pallas_call(functools.partial(fused_kernel, n_rows, n_cols, cap, rb, c...  339 us
  transfers between devices with their start and end apart: 1, of which 0 were waited for; matrix products, arithmetic and copies ran while one was open for 3% of the time, Pallas kernels for 0%

profile of v2, /device:TPU:0, one launch (start us, length us, event | category | flops | bytes accessed | tf_op | source)
XLA Modules:
  0.0 371.8 jit_solution(6473263665309243231)
XLA Ops:
  0.0 0.9 fusion.4
  0.9 0.9 fusion.8
  1.8 0.2 convert_reduce_fusion
  2.0 0.8 fusion.5
  2.7 0.8 fusion.9
  3.5 0.2 convert_reduce_fusion.1
  3.7 0.6 select_reduce_fusion.4
  4.4 0.1 copy.23
  4.5 0.6 select_reduce_fusion.2
  5.6 0.7 copy.24
  6.2 7.3 %all-to-all-start = ((s32[32,1,32]{2,1,0:T(1,128)}), s32[32,1,32]{2,1,0:T(1,128)S(1)}, u32[]{:S(2)}, u32[]{:S(2)}) async-start(s32[32,1,32]{2,1,0:T(1,128)} %copy.24), calls=%async_computation | async-start | bytes 32768 | tf_op jit(solution)/shard_map/all_to_all | solution.py:324
  13.5 0.6 broadcast_maximum_fusion.1
  14.1 0.7 broadcast_maximum_fusion
  14.8 0.7 convert_element_type.11
  15.6 0.7 copy.30
  16.3 3.6 gather_fusion.1
  19.9 3.1 gather_fusion
  23.2 0.6 slice_bitcast_fusion
  23.9 1.1 copy.27
  25.0 0.1 eq.116
  25.1 1.1 copy.26
  26.4 0.8 select_reduce_fusion
  27.2 338.7 %shard_map.55 = bf16[1792,1792]{1,0:T(8,128)(2,1)} custom-call(s32[4,112]{1,0:T(4,128)} %get-tuple-element.18.a_index, s32[4,112]{1,0:T(4,128)} %get-tuple-element.17.b_index, bf16[4,8,4,128,128]{4,3,2,1,0:T(8,128)(2,1)} %bitcast.76, bf16[4,4,4,128,128]{4,3,2,1,0:T(8,128)(2,1)} %bitcast.77, f32[14,1792]{1,0:T(8,128)} %bitcast.79), custom_call_target="tpu_custom_call" | custom-call | tf_op jit(solution)/shard_map/pallas_call | solution.py:338
  365.8 6.0 %copy.32 = bf16[1792,1792]{1,0:T(8,128)(2,1)} copy(bf16[1792,1792]{1,0:T(8,128)(2,1)} %shard_map.55) | data formatting | bytes 12845056
  (19 shorter events, 0.9 us)
Async XLA Ops:
  0.0 19.9 %copy-start = (bf16[104,128,128]{2,1,0:T(8,128)(2,1)S(1)}, bf16[104,128,128]{2,1,0:T(8,128)(2,1)}, u32[]{:S(2)}) copy-start(bf16[104,128,128]{2,1,0:T(8,128)(2,1)} %param.5) | copy-start | bytes 10223620
  6.2 16.8 %all-to-all-start = ((s32[32,1,32]{2,1,0:T(1,128)}), s32[32,1,32]{2,1,0:T(1,128)S(1)}, u32[]{:S(2)}, u32[]{:S(2)}) async-start(s32[32,1,32]{2,1,0:T(1,128)} %copy.24), calls=%async_computation | async-start | bytes 32768 | tf_op jit(solution)/shard_map/all_to_all | solution.py:324

commit v3 on v2

--- a/solution.py
+++ b/solution.py
@@ -211,10 +211,33 @@
                     def _():
                         az(p, hop, way).start()
 
-    def multiply(p):
+    def lay_b(p):
         for d in range(1, n_rows):
             bx(p, d).wait_recv()
 
+        def place_b(k, carry):
+            rows = pl.ds(pl.multiple_of(k * bs, bs), bs)
+            for j in range(cb):
+                b_dense[rows, j * bs:(j + 1) * bs] = b_parts[p][b_index[p, k * cb + j]]
+            return carry
+
+        lax.fori_loop(0, KB, place_b, 0)
+
+    wide = 2 * bs
+    high = rb // 2
+    tall = high * bs
+    tiles = 2 * (cb * bs // wide)
+
+    def tile_at(t):
+        rows = pl.ds(pl.multiple_of((t % 2) * tall, tall), tall)
+        cols = pl.ds(pl.multiple_of((t // 2) * wide, wide), wide)
+        return rows, cols
+
+    def finish(t):
+        rows, cols = tile_at(t)
+        return pltpu.make_async_copy(stage.at[rows, cols], out.at[rows, cols], out_sem.at[t])
+
+    def multiply(p):
         def place_a(i, carry):
             rows = pl.ds(pl.multiple_of(i * bs, bs), bs)
             for k in range(KB):
@@ -223,25 +246,22 @@
 
         lax.fori_loop(0, rb, place_a, 0)
 
-        def place_b(k, carry):
-            rows = pl.ds(pl.multiple_of(k * bs, bs), bs)
-            for j in range(cb):
-                b_dense[rows, j * bs:(j + 1) * bs] = b_parts[p][b_index[p, k * cb + j]]
+        def tile(t, carry):
+            rows, cols = tile_at(t)
+            term = jnp.dot(a_dense[rows, :], b_dense[:, cols], preferred_element_type=jnp.float32)
+            if p > 0:
+                term = acc[rows, cols] + term
+            if p + 1 < n_cols:
+                acc[rows, cols] = term
+                return carry
+            for i in range(high):
+                top = pl.multiple_of((t % 2) * tall + i * bs, bs)
+                kept = keep[pl.ds((t % 2) * high + i, 1), cols]
+                stage[pl.ds(top, bs), cols] = (term[i * bs:(i + 1) * bs] * kept).astype(jnp.bfloat16)
+            finish(t).start()
             return carry
 
-        lax.fori_loop(0, KB, place_b, 0)
-
-        wide = 2 * bs
-        tall = rb * bs // 2
-
-        def tile(t, carry):
-            rows = pl.ds(pl.multiple_of((t % 2) * tall, tall), tall)
-            cols = pl.ds(pl.multiple_of((t // 2) * wide, wide), wide)
-            term = jnp.dot(a_dense[rows, :], b_dense[:, cols], preferred_element_type=jnp.float32)
-            acc[rows, cols] = term if p == 0 else acc[rows, cols] + term
-            return carry
-
-        lax.fori_loop(0, 2 * (cb * bs // wide), tile, 0)
+        lax.fori_loop(0, tiles, tile, 0)
 
     for p in range(n_cols):
         for d in range(1, n_rows):
@@ -258,18 +278,10 @@
     for p in range(n_cols):
         if p + 1 < n_cols:
             open_part(p + 1)
+        lay_b(p)
         relay(p)
         multiply(p)
 
-    def finish(i):
-        return pltpu.make_async_copy(
-            stage.at[i * bs:(i + 1) * bs], out.at[i * bs:(i + 1) * bs], out_sem.at[i]
-        )
-
-    for i in range(rb):
-        rows = slice(i * bs, (i + 1) * bs)
-        stage[rows, :] = (acc[rows, :] * keep[i:i + 1, :]).astype(jnp.bfloat16)
-        finish(i).start()
     for p in range(n_cols):
         for d in range(1, n_rows):
             ax(p, d).wait_send()
@@ -281,8 +293,12 @@
                 @pl.when(can_send(hop, way))
                 def _():
                     az(p, hop, way).wait_send()
-    for i in range(rb):
-        finish(i).wait()
+
+    def settle(t, carry):
+        finish(t).wait()
+        return carry
+
+    lax.fori_loop(0, tiles, settle, 0)
 
 
 def slot_sources(owner, count, cap):
@@ -362,7 +378,7 @@
             dma((n_cols, n_cols - 1, 2)),
             dma((n_cols, n_cols - 1, 2)),
             dma((2, n_cols)),
-            dma((rb,)),
+            dma((2 * (cb // 2),)),
         ],
         compiler_params=pltpu.CompilerParams(
             collective_id=0, has_side_effects=True, vmem_limit_bytes=60 * 2**20

time: 372 us -> 367 us (0.987)
  Pallas kernels: 339 us -> 331 us
    pallas_call x1, Pallas kernels: 339 us -> 331 us  [gathered(): pl.pallas_call(functools.partial(fused_kernel, n_rows, n_cols, cap, rb, c...]
where the time goes in v3:
time: 367 us; the launch traced here: 364 us
  Pallas kernels  331 us (90%)
  local copies, waits for them, and re-layouts  18.1 us (5%)
  other arithmetic  7.71 us (2%)
  starting transfers between devices  7.3 us (2%)
    pallas_call x1, Pallas kernels, gathered(): pl.pallas_call(functools.partial(fused_kernel, n_rows, n_cols, cap, rb, c...  331 us
  transfers between devices with their start and end apart: 1, of which 0 were waited for; matrix products, arithmetic and copies ran while one was open for 3% of the time, Pallas kernels for 0%

profile of v3, /device:TPU:0, one launch (start us, length us, event | category | flops | bytes accessed | tf_op | source)
XLA Modules:
  0.0 364.2 jit_solution(2104115472334224321)
XLA Ops:
  0.0 0.9 fusion.4
  0.9 0.9 fusion.8
  1.8 0.2 convert_reduce_fusion
  2.0 0.8 fusion.5
  2.7 0.8 fusion.9
  3.5 0.2 convert_reduce_fusion.1
  3.7 0.6 select_reduce_fusion.4
  4.4 0.1 copy.23
  4.5 0.6 select_reduce_fusion.2
  5.6 0.7 copy.24
  6.2 7.3 %all-to-all-start = ((s32[32,1,32]{2,1,0:T(1,128)}), s32[32,1,32]{2,1,0:T(1,128)S(1)}, u32[]{:S(2)}, u32[]{:S(2)}) async-start(s32[32,1,32]{2,1,0:T(1,128)} %copy.24), calls=%async_computation | async-start | bytes 32768 | tf_op jit(solution)/shard_map/all_to_all | solution.py:340
  13.5 0.6 broadcast_maximum_fusion.1
  14.1 0.7 broadcast_maximum_fusion
  14.8 0.7 convert_element_type.11
  15.6 0.7 copy.30
  16.3 3.6 gather_fusion.1
  19.9 3.1 gather_fusion
  23.2 0.6 slice_bitcast_fusion
  23.9 1.1 copy.27
  25.0 0.1 eq.116
  25.1 1.1 copy.26
  26.4 0.8 select_reduce_fusion
  27.2 331.0 %shard_map.55 = bf16[1792,1792]{1,0:T(8,128)(2,1)} custom-call(s32[4,112]{1,0:T(4,128)} %get-tuple-element.18.a_index, s32[4,112]{1,0:T(4,128)} %get-tuple-element.17.b_index, bf16[4,8,4,128,128]{4,3,2,1,0:T(8,128)(2,1)} %bitcast.76, bf16[4,4,4,128,128]{4,3,2,1,0:T(8,128)(2,1)} %bitcast.77, f32[14,1792]{1,0:T(8,128)} %bitcast.79), custom_call_target="tpu_custom_call" | custom-call | tf_op jit(solution)/shard_map/pallas_call | solution.py:354
  358.2 6.0 %copy.32 = bf16[1792,1792]{1,0:T(8,128)(2,1)} copy(bf16[1792,1792]{1,0:T(8,128)(2,1)} %shard_map.55) | data formatting | bytes 12845056
  (19 shorter events, 0.9 us)
Async XLA Ops:
  0.0 19.9 %copy-start = (bf16[104,128,128]{2,1,0:T(8,128)(2,1)S(1)}, bf16[104,128,128]{2,1,0:T(8,128)(2,1)}, u32[]{:S(2)}) copy-start(bf16[104,128,128]{2,1,0:T(8,128)(2,1)} %param.5) | copy-start | bytes 10223620
  6.2 16.8 %all-to-all-start = ((s32[32,1,32]{2,1,0:T(1,128)}), s32[32,1,32]{2,1,0:T(1,128)S(1)}, u32[]{:S(2)}, u32[]{:S(2)}) async-start(s32[32,1,32]{2,1,0:T(1,128)} %copy.24), calls=%async_computation | async-start | bytes 32768 | tf_op jit(solution)/shard_map/all_to_all | solution.py:340
